TPU v7x, 256 devices: a whole 4x4x8 slice. The times are simulated.
256 devices in a mesh: grp: 8 (over x, z_lo), ref: 32 (over z_hi, y, core).
Axes of the slice: x: 4, y: 4, z: 8 (z_hi: 4, z_lo: 2; z = z_hi * 2 + z_lo), core: 2. Of those that a mesh axis runs over, the one named last changes fastest.
Arguments:
- particles: bfloat16 [2048, 512], P(('grp', 'ref')), may hold values from -30 to 30
- samples: bfloat16 [131072, 512], P('ref'), may hold values from -6 to 6
Outputs:
- moved: float32 [2048, 512], P(('grp', 'ref'))
All inputs are finite; a program needn't handle non-finite values.
Results may differ from a plain program's by a relative error of at most 0.0035.
Values may be sent and summed in bfloat16 or wider, within the bound.
A program may use at most 128 MiB of HBM per device.

v0:
```python
import jax
import jax.numpy as jnp
from jax import lax
from jax.sharding import PartitionSpec as P

KERNEL_WIDTH = 16
step_size = 8.0
masked_score = -1e30


def combined_all(part, axis, combine):
    gathered = jax.tree.map(lambda a: lax.all_gather(a, axis), part)

    def take(source):
        return jax.tree.map(lambda a: lax.dynamic_index_in_dim(a, source, 0, False), gathered)

    return lax.fori_loop(
        1, lax.axis_size(axis), lambda source, state: combine(state, take(source)), take(0)
    )


def square_norms(values):
    wide = values.astype(jnp.float32)
    return jnp.sum(wide * wide, axis=1)


def row_terms(row_block, row_sq, row_ids, samples, ref_sq, columns, column_sq, column_ids):
    cross_scores = (
        2.0 * jnp.einsum("rd,md->rm", row_block, samples, preferred_element_type=jnp.float32)
        - row_sq[:, None]
        - ref_sq[None, :]
    ) / (2.0 * KERNEL_WIDTH)
    cross_max = jnp.max(cross_scores, axis=1)
    cross_weights = jnp.exp(cross_scores - cross_max[:, None])
    cross_total = jnp.sum(cross_weights, axis=1)
    cross_sum = jnp.dot(
        cross_weights.astype(jnp.bfloat16), samples, preferred_element_type=jnp.float32
    )
    self_scores = (
        2.0 * jnp.einsum("rd,cd->rc", row_block, columns, preferred_element_type=jnp.float32)
        - row_sq[:, None]
        - column_sq[None, :]
    ) / (2.0 * KERNEL_WIDTH)
    diag_mask = row_ids[:, None] == column_ids[None, :]
    self_scores = jnp.where(diag_mask, masked_score, self_scores)
    self_max = jnp.max(self_scores, axis=1)
    self_weights = jnp.where(diag_mask, 0.0, jnp.exp(self_scores - self_max[:, None]))
    self_total = jnp.sum(self_weights, axis=1)
    self_sum = jnp.dot(
        self_weights.astype(jnp.bfloat16), columns, preferred_element_type=jnp.float32
    )
    return (cross_max, cross_total, cross_sum, self_max, self_total, self_sum)


def combine_parts(left_side, right_side):
    cross_top = jnp.maximum(left_side[0], right_side[0])
    left_cross = jnp.exp(left_side[0] - cross_top)
    right_cross = jnp.exp(right_side[0] - cross_top)
    self_top = jnp.maximum(left_side[3], right_side[3])
    left_self = jnp.exp(left_side[3] - self_top)
    right_self = jnp.exp(right_side[3] - self_top)
    return (
        cross_top,
        left_side[1] * left_cross + right_side[1] * right_cross,
        left_side[2] * left_cross[:, None] + right_side[2] * right_cross[:, None],
        self_top,
        left_side[4] * left_self + right_side[4] * right_self,
        left_side[5] * left_self[:, None] + right_side[5] * right_self[:, None],
    )


def per_device(particles, samples):
    part_dev = particles.shape[0]
    grp_count = lax.axis_size("grp")
    grp_pos = lax.axis_index("grp")
    ref_pos = lax.axis_index("ref")
    group = lax.all_gather(particles, "ref", axis=0, tiled=True)
    columns = lax.all_gather(particles, "grp", axis=0, tiled=True)
    group_rows = group.shape[0]
    column_ids = (
        jnp.arange(grp_count, dtype=jnp.int32)[:, None] * group_rows
        + ref_pos * part_dev
        + jnp.arange(part_dev, dtype=jnp.int32)[None, :]
    ).reshape(-1)
    row_ids = grp_pos * group_rows + jnp.arange(group_rows, dtype=jnp.int32)
    group_sq = square_norms(group)
    column_sq = square_norms(columns)
    ref_sq = square_norms(samples)
    block_rows = min(512, group_rows)
    blocks = group_rows // block_rows

    def one_block(inputs):
        row_block, row_sq, block_ids = inputs
        return row_terms(
            row_block, row_sq, block_ids, samples, ref_sq, columns, column_sq, column_ids
        )

    stacked_terms = lax.map(
        one_block,
        (
            group.reshape(blocks, block_rows, group.shape[1]),
            group_sq.reshape(blocks, block_rows),
            row_ids.reshape(blocks, block_rows),
        ),
    )
    cross_max, cross_total, cross_sum, self_max, self_total, self_sum = tuple(
        (stacked.reshape((group_rows,) + stacked.shape[2:]) for stacked in stacked_terms)
    )
    merged = combined_all(
        (cross_max, cross_total, cross_sum, self_max, self_total, self_sum), "ref", combine_parts
    )
    start = ref_pos * part_dev
    cross_mean = (
        lax.dynamic_slice_in_dim(merged[2], start, part_dev, 0)
        / lax.dynamic_slice_in_dim(merged[1], start, part_dev, 0)[:, None]
    )
    self_mean = (
        lax.dynamic_slice_in_dim(merged[5], start, part_dev, 0)
        / lax.dynamic_slice_in_dim(merged[4], start, part_dev, 0)[:, None]
    )
    return particles.astype(jnp.float32) + step_size * (cross_mean - self_mean)


def solution(mesh):
    in_specs = (P(("grp", "ref"), None), P("ref", None))
    out_specs = P(("grp", "ref"), None)
    return jax.shard_map(
        per_device, mesh=mesh, in_specs=in_specs, out_specs=out_specs, check_vma=False
    )
```

profile of v0, /device:TPU:3, one launch (start us, length us, event | category | flops | bytes accessed | tf_op | source)
XLA Modules:
  0.0 376.9 jit_solution(6727869570558348518)
XLA Ops:
  6.5 0.0 all-gather.15.cloned.1.call-start
  6.5 20.5 %all_gather.28 = bf16[64,512]{1,0:T(8,128)(2,1)S(1)} all-gather(bf16[8,512]{1,0:T(8,128)(2,1)} %param.4), channel_id=1, replica_groups=mesh['grp'=8,'ref'=32] {'grp'}, dimensions={0}, use_global_device_ids=true | all-gather | bytes 73728 | tf_op jit(solution)/shard_map/all_gather | solution.py:78
  27.0 54.9 %all_gather.24 = bf16[256,512]{1,0:T(8,128)(2,1)S(1)} all-gather(bf16[8,512]{1,0:T(8,128)(2,1)} %param.4), channel_id=1, replica_groups=mesh['grp'=8,'ref'=32] {'ref'}, dimensions={0}, use_global_device_ids=true | all-gather | bytes 270336 | tf_op jit(solution)/shard_map/all_gather | solution.py:77
  81.9 0.1 iota_add_fusion
  82.0 0.1 add.141
  82.1 0.1 multiply_reduce_fusion.2
  82.2 0.1 multiply_reduce_fusion.1
  82.3 0.2 fusion.24
  82.5 1.1 fusion.16
  83.7 0.0 all-gather.15.cloned.1.call-update
  83.7 0.0 all-gather.13.cloned.1.call-start
  83.7 0.0 copy-start
  83.8 3.2 multiply_reduce_fusion
  87.0 0.2 copy-done
  87.2 1.4 fusion.23
  88.7 2.0 copy-done.1
  90.7 2.1 fusion.7
  92.8 0.0 all-gather.13.cloned.1.call-update
  92.8 0.1 fusion.15
  92.9 40.8 %all-gather.9 = f32[32,1,256]{2,1,0:T(1,128)S(1)} all-gather(f32[1,1,256]{2,1,0:T(1,128)S(1)} %bitcast.65), channel_id=6, replica_groups=mesh['grp'=8,'ref'=32] {'ref'}, dimensions={0}, use_global_device_ids=true | all-gather | bytes 33792 | tf_op jit(solution)/shard_map/all_gather | solution.py:12
  133.8 44.0 %all-gather.8 = f32[32,1,256]{2,1,0:T(1,128)S(1)} all-gather(f32[1,1,256]{2,1,0:T(1,128)S(1)} %bitcast.64), channel_id=5, replica_groups=mesh['grp'=8,'ref'=32] {'ref'}, dimensions={0}, use_global_device_ids=true | all-gather | bytes 33792 | tf_op jit(solution)/shard_map/all_gather | solution.py:12
  177.8 3.1 fusion.6
  180.9 39.5 %all-gather.7 = f32[32,1,256]{2,1,0:T(1,128)S(1)} all-gather(f32[1,1,256]{2,1,0:T(1,128)S(1)} %bitcast.67), channel_id=3, replica_groups=mesh['grp'=8,'ref'=32] {'ref'}, dimensions={0}, use_global_device_ids=true | all-gather | bytes 33792 | tf_op jit(solution)/shard_map/all_gather | solution.py:12
  220.4 40.3 %all-gather.6 = f32[32,1,256]{2,1,0:T(1,128)S(1)} all-gather(f32[1,1,256]{2,1,0:T(1,128)S(1)} %bitcast.66), channel_id=2, replica_groups=mesh['grp'=8,'ref'=32] {'ref'}, dimensions={0}, use_global_device_ids=true | all-gather | bytes 33792 | tf_op jit(solution)/shard_map/all_gather | solution.py:12
  260.7 1.1 slice.21
  261.8 56.3 %all-gather.13.cloned.1.call-done = f32[8192,512]{1,0:T(8,128)} async-done(((f32[256,512]{1,0:T(8,128)}), f32[8192,512]{1,0:T(8,128)}) %all-gather.13.cloned.1.call-update) | async-done | bytes 16777232 | tf_op jit(solution)/shard_map/all_gather | solution.py:12
  318.1 1.1 slice.18
  319.2 0.0 copy-start.2
  319.2 50.0 %while.6 = (s32[]{:T(128)}, f32[256]{0:T(256)S(1)}, f32[256]{0:T(256)S(1)}, f32[256,512]{1,0:T(8,128)S(1)}, f32[256]{0:T(256)S(1)}, /*index=5*/f32[256]{0:T(256)...) while((s32[]{:T(128)}, f32[256]{0:T(256)S(1)}, ...), condition=%wide.region_8.9_spmd, body=%wide.region_7.8_spmd.sunk | while | flops 789509 | bytes 3174603 | solution.py:17
  319.3 1.5 fusion.32
  320.9 1.5 fusion.32
  322.5 1.5 fusion.32
  324.2 1.5 fusion.32
  325.8 1.5 fusion.32
  327.4 1.5 fusion.32
  329.0 1.5 fusion.32
  330.6 1.5 fusion.32
  332.2 1.5 fusion.32
  333.8 1.5 fusion.32
  335.4 1.5 fusion.32
  337.1 1.5 fusion.32
  338.7 1.5 fusion.32
  340.3 1.5 fusion.32
  341.9 1.5 fusion.32
  343.5 1.5 fusion.32
  345.1 1.5 fusion.32
  346.8 1.5 fusion.32
  348.4 1.5 fusion.32
  350.0 1.5 fusion.32
  351.6 1.5 fusion.32
  353.2 1.5 fusion.32
  354.8 1.5 fusion.32
  356.4 1.5 fusion.32
  358.0 1.5 fusion.32
  359.7 1.5 fusion.32
  361.3 1.5 fusion.32
  362.9 1.5 fusion.32
  364.5 1.5 fusion.32
  366.1 1.5 fusion.32
  367.7 1.5 fusion.32
  369.2 0.1 dynamic_slice.110
  369.3 0.1 dynamic_slice.108
  369.4 0.0 copy-done.2
  369.4 0.7 multiply_add_fusion.2
  (198 shorter events, 2.7 us)
Async XLA Ops:
  6.5 254.2 %all-gather.15.cloned.1.call-start = ((), (), s32[]{:S(2)}) async-start(), calls=%async_computation.1 | async-start | bytes 17301504 | tf_op jit(solution)/shard_map/all_gather | solution.py:12
  83.7 234.4 %all-gather.13.cloned.1.call-start = ((), (), s32[]{:S(2)}) async-start(), calls=%async_computation | async-start | bytes 17301504 | tf_op jit(solution)/shard_map/all_gather | solution.py:12
  83.7 3.5 copy-start
  88.6 2.1 copy-start.1
  319.2 50.2 %copy-start.2 = (bf16[8,512]{1,0:T(8,128)(2,1)S(1)}, bf16[8,512]{1,0:T(8,128)(2,1)}, u32[]{:S(2)}) copy-start(bf16[8,512]{1,0:T(8,128)(2,1)} %param.4) | copy-start | bytes 24580
Sparse Core Ops, SparseCore 0:
  83.8 114.7 all-gather.14
  201.2 116.8 all-gather.12
where the time goes:
time: 378 us; the launch traced here: 377 us
  blocking collectives  240 us (63%)
  waiting for transfers between devices  56.3 us (15%)
  other arithmetic  54.2 us (14%)
  between operations  13.5 us (4%)
  local copies, waits for them, and re-layouts  6.1 us (2%)
  matrix products  4.92 us (1%)
    all_gather x4, blocking collectives, combined_all(): gathered = jax.tree.map(lambda a: lax.all_gather(a, axis), part)  165 us
    all_gather x2, waiting for transfers between devices, combined_all(): gathered = jax.tree.map(lambda a: lax.all_gather(a, axis), part)  56.3 us
    all_gather x1, blocking collectives, per_device(): group = lax.all_gather(particles, 'ref', axis=0, tiled=True)  54.9 us
    add x31, other arithmetic, combine_parts(): left_side[5] * left_self[:, None] + right_side[5] * right_self[:, None]  45.5 us
    all_gather x1, blocking collectives, per_device(): columns = lax.all_gather(particles, 'grp', axis=0, tiled=True)  20.5 us
  transfers between devices with their start and end apart: 2, of which 1 were waited for; matrix products, arithmetic and copies ran while one was open for 3% of the time, Pallas kernels for 0%

commit v1 on v0

--- a/solution.py
+++ b/solution.py
@@ -74,7 +74,9 @@
     grp_count = lax.axis_size("grp")
     grp_pos = lax.axis_index("grp")
     ref_pos = lax.axis_index("ref")
-    group = lax.all_gather(particles, "ref", axis=0, tiled=True)
+    group = jnp.concatenate(
+        lax.all_to_all(jnp.stack([particles] * lax.axis_size("ref")), "ref", 0, 0), axis=0
+    )
     columns = lax.all_gather(particles, "grp", axis=0, tiled=True)
     group_rows = group.shape[0]
     column_ids = (

time: 378 us -> 350 us (0.926); the launches traced: 377 us -> 344 us
  blocking collectives: 240 us -> 200 us
  starting transfers between devices: 0.04 us -> 12 us
  waiting for transfers between devices: 56.3 us -> 50.1 us
    all_gather x1 -> x0, blocking collectives: 54.9 us -> none  [per_device(): group = lax.all_gather(particles, 'ref', axis=0, tiled=True)]
    all_gather x4, blocking collectives: 165 us -> 177 us  [combined_all(): gathered = jax.tree.map(lambda a: lax.all_gather(a, axis), part)]
    all_to_all x0 -> x1, starting transfers between devices: none -> 11.9 us  [per_device(): lax.all_to_all(jnp.stack([particles] * lax.axis_size('ref')), 'ref', 0, 0)]
    all_gather x2, waiting for transfers between devices: 56.3 us -> 50.1 us  [combined_all(): gathered = jax.tree.map(lambda a: lax.all_gather(a, axis), part)]
  transfers between devices with their start and end apart: 2 -> 3, of which waited for: 1 -> 1; matrix products, arithmetic and copies ran while one was open for 3% -> 3% of each run, Pallas kernels for 0% -> 0%
where the time goes in v1:
time: 350 us; the launch traced here: 344 us
  blocking collectives  200 us (57%)
  other arithmetic  54.2 us (15%)
  waiting for transfers between devices  50.1 us (14%)
  between operations  13.5 us (4%)
  starting transfers between devices  12 us (3%)
  local copies, waits for them, and re-layouts  7.61 us (2%)
  matrix products  4.91 us (1%)
    all_gather x4, blocking collectives, combined_all(): gathered = jax.tree.map(lambda a: lax.all_gather(a, axis), part)  177 us
    all_gather x2, waiting for transfers between devices, combined_all(): gathered = jax.tree.map(lambda a: lax.all_gather(a, axis), part)  50.1 us
    add x31, other arithmetic, combine_parts(): left_side[5] * left_self[:, None] + right_side[5] * right_self[:, None]  45.5 us
    all_gather x1, blocking collectives, per_device(): columns = lax.all_gather(particles, 'grp', axis=0, tiled=True)  22.9 us
    all_to_all x1, starting transfers between devices, per_device(): lax.all_to_all(jnp.stack([particles] * lax.axis_size('ref')), 'ref', 0, 0)  11.9 us
  transfers between devices with their start and end apart: 3, of which 1 were waited for; matrix products, arithmetic and copies ran while one was open for 3% of the time, Pallas kernels for 0%

profile of v1, /device:TPU:3, one launch (start us, length us, event | category | flops | bytes accessed | tf_op | source)
XLA Modules:
  0.0 344.5 jit_solution(7723811195916477412)
XLA Ops:
  6.5 1.4 stack.2
  7.9 11.9 %all-to-all-start = ((bf16[32,8,512]{2,1,0:T(8,128)(2,1)}), bf16[32,8,512]{2,1,0:T(8,128)(2,1)S(1)}, u32[]{:S(2)}, u32[]{:S(2)}) async-start(bf16[32,8,512]{2,1,0:T(8,128)(2,1)} %stack.2), calls=%async_computation | async-start | bytes 524288 | tf_op jit(solution)/shard_map/all_to_all | solution.py:78
  19.9 0.0 all-gather.15.cloned.1.call-start
  19.9 0.1 iota_add_fusion
  20.0 0.1 add.141
  20.1 22.9 %all_gather.24 = bf16[64,512]{1,0:T(8,128)(2,1)S(1)} all-gather(bf16[8,512]{1,0:T(8,128)(2,1)} %param.4), channel_id=1, replica_groups=mesh['grp'=8,'ref'=32] {'grp'}, dimensions={0}, use_global_device_ids=true | all-gather | bytes 73728 | tf_op jit(solution)/shard_map/all_gather | solution.py:80
  43.0 0.1 multiply_reduce_fusion.2
  43.1 0.1 multiply_reduce_fusion.1
  43.2 0.1 sub.115
  43.3 0.2 fusion.26
  43.5 1.1 fusion.18
  44.7 0.0 all-gather.15.cloned.1.call-update
  44.7 0.0 all-gather.13.cloned.1.call-start
  44.8 3.2 multiply_reduce_fusion
  48.0 0.2 copy-done
  48.2 1.4 fusion.25
  49.6 2.0 copy-done.1
  51.7 2.1 fusion.7
  53.8 0.0 all-gather.13.cloned.1.call-update
  53.8 0.1 fusion.17
  53.9 52.3 %all-gather.9 = f32[32,1,256]{2,1,0:T(1,128)S(1)} all-gather(f32[1,1,256]{2,1,0:T(1,128)S(1)} %bitcast.72), channel_id=6, replica_groups=mesh['grp'=8,'ref'=32] {'ref'}, dimensions={0}, use_global_device_ids=true | all-gather | bytes 33792 | tf_op jit(solution)/shard_map/all_gather | solution.py:12
  106.2 42.0 %all-gather.8 = f32[32,1,256]{2,1,0:T(1,128)S(1)} all-gather(f32[1,1,256]{2,1,0:T(1,128)S(1)} %bitcast.71), channel_id=5, replica_groups=mesh['grp'=8,'ref'=32] {'ref'}, dimensions={0}, use_global_device_ids=true | all-gather | bytes 33792 | tf_op jit(solution)/shard_map/all_gather | solution.py:12
  148.2 3.1 fusion.6
  151.3 42.7 %all-gather.7 = f32[32,1,256]{2,1,0:T(1,128)S(1)} all-gather(f32[1,1,256]{2,1,0:T(1,128)S(1)} %bitcast.74), channel_id=3, replica_groups=mesh['grp'=8,'ref'=32] {'ref'}, dimensions={0}, use_global_device_ids=true | all-gather | bytes 33792 | tf_op jit(solution)/shard_map/all_gather | solution.py:12
  194.0 40.5 %all-gather.6 = f32[32,1,256]{2,1,0:T(1,128)S(1)} all-gather(f32[1,1,256]{2,1,0:T(1,128)S(1)} %bitcast.73), channel_id=2, replica_groups=mesh['grp'=8,'ref'=32] {'ref'}, dimensions={0}, use_global_device_ids=true | all-gather | bytes 33792 | tf_op jit(solution)/shard_map/all_gather | solution.py:12
  234.5 1.1 slice.21
  235.6 50.1 %all-gather.13.cloned.1.call-done = f32[8192,512]{1,0:T(8,128)} async-done(((f32[256,512]{1,0:T(8,128)}), f32[8192,512]{1,0:T(8,128)}) %all-gather.13.cloned.1.call-update) | async-done | bytes 16777232 | tf_op jit(solution)/shard_map/all_gather | solution.py:12
  285.7 1.1 slice.18
  286.8 0.0 copy-start.2
  286.8 50.0 %while.6 = (s32[]{:T(128)}, f32[256]{0:T(256)S(1)}, f32[256]{0:T(256)S(1)}, f32[256,512]{1,0:T(8,128)S(1)}, f32[256]{0:T(256)S(1)}, /*index=5*/f32[256]{0:T(256)...) while((s32[]{:T(128)}, f32[256]{0:T(256)S(1)}, ...), condition=%wide.region_8.9_spmd, body=%wide.region_7.8_spmd.sunk | while | flops 789509 | bytes 3174603 | solution.py:17
  286.9 1.5 fusion.32
  288.5 1.5 fusion.32
  290.1 1.5 fusion.32
  291.7 1.5 fusion.32
  293.4 1.5 fusion.32
  295.0 1.5 fusion.32
  296.6 1.5 fusion.32
  298.2 1.5 fusion.32
  299.8 1.5 fusion.32
  301.4 1.5 fusion.32
  303.0 1.5 fusion.32
  304.6 1.5 fusion.32
  306.3 1.5 fusion.32
  307.9 1.5 fusion.32
  309.5 1.5 fusion.32
  311.1 1.5 fusion.32
  312.7 1.5 fusion.32
  314.3 1.5 fusion.32
  316.0 1.5 fusion.32
  317.6 1.5 fusion.32
  319.2 1.5 fusion.32
  320.8 1.5 fusion.32
  322.4 1.5 fusion.32
  324.0 1.5 fusion.32
  325.6 1.5 fusion.32
  327.2 1.5 fusion.32
  328.9 1.5 fusion.32
  330.5 1.5 fusion.32
  332.1 1.5 fusion.32
  333.7 1.5 fusion.32
  335.3 1.5 fusion.32
  336.8 0.1 dynamic_slice.110
  336.9 0.1 dynamic_slice.108
  336.9 0.7 multiply_add_fusion.2
  (201 shorter events, 2.7 us)
Async XLA Ops:
  7.9 35.1 %all-to-all-start = ((bf16[32,8,512]{2,1,0:T(8,128)(2,1)}), bf16[32,8,512]{2,1,0:T(8,128)(2,1)S(1)}, u32[]{:S(2)}, u32[]{:S(2)}) async-start(bf16[32,8,512]{2,1,0:T(8,128)(2,1)} %stack.2), calls=%async_computation | async-start | bytes 524288 | tf_op jit(solution)/shard_map/all_to_all | solution.py:78
  19.9 214.6 %all-gather.15.cloned.1.call-start = ((), (), s32[]{:S(2)}) async-start(), calls=%async_computation.2 | async-start | bytes 17301504 | tf_op jit(solution)/shard_map/all_gather | solution.py:12
  44.7 241.0 %all-gather.13.cloned.1.call-start = ((), (), s32[]{:S(2)}) async-start(), calls=%async_computation.1 | async-start | bytes 17301504 | tf_op jit(solution)/shard_map/all_gather | solution.py:12
  44.7 3.5 %copy-start = (bf16[4096,512]{1,0:T(8,128)(2,1)S(1)}, bf16[4096,512]{1,0:T(8,128)(2,1)}, u32[]{:S(2)}) copy-start(bf16[4096,512]{1,0:T(8,128)(2,1)} %param.5) | copy-start | bytes 12582916
  49.6 2.1 copy-start.1
  286.8 50.2 %copy-start.2 = (bf16[8,512]{1,0:T(8,128)(2,1)S(1)}, bf16[8,512]{1,0:T(8,128)(2,1)}, u32[]{:S(2)}) copy-start(bf16[8,512]{1,0:T(8,128)(2,1)} %param.4) | copy-start | bytes 24580
Sparse Core Ops, SparseCore 0:
  44.8 117.5 all-gather.14
  165.0 120.6 all-gather.12
